TPU v7x, 32 devices: a whole 2x2x4 slice. The times are simulated.
32 devices in a mesh: dp: 8 (over z, x), latent: 4 (over y, core).
Axes of the slice: x: 2, y: 2, z: 4, core: 2. Of those that a mesh axis runs over, the one named last changes fastest.
Arguments:
- tokens: bfloat16 [1024, 1536], P('dp'), may hold values from -6 to 6
- enc_weight: bfloat16 [1536, 32768], P(None, ('dp', 'latent')), may hold values from -0.15625 to 0.15625
- enc_bias: float32 [32768], P(('dp', 'latent')), may hold values from -3 to 3
- dec_weight: bfloat16 [32768, 1536], P(('dp', 'latent')), may hold values from -0.0625 to 0.0625
- dec_bias: float32 [1536], replicated, may hold values from -3 to 3
- slot_token: int32 [1024], P(('dp', 'latent')), may hold values from 0 to 7
- slot_latent: int32 [1024], P(('dp', 'latent')), may hold values from 0 to 7
- slot_count: int32 [32], P(('dp', 'latent')), may hold values from 6 to 32, as said below
Outputs:
- enc_grad: bfloat16 [1536, 32768], P(None, ('dp', 'latent'))
- dec_grad: bfloat16 [32768, 1536], P(('dp', 'latent'))
- enc_bias_grad: float32 [32768], P(('dp', 'latent'))
- dec_bias_grad: float32 [1536], replicated
- mean_error: float32 [], replicated
Inputs may be any that keep to these rules, and one draw needn't show every extreme that they name: `slot_count`: slot lists of one device never repeat a (token block, latent block) pair among its 32 slots; entries past a device's count name valid blocks and are ignored; some device has all 32 slots live in every draw.
All inputs are finite; a program needn't handle non-finite values.
Results may differ from a plain program's by a relative error of at most 0.0065.
Values may be sent and summed in bfloat16 or wider, within the bound.
A program may use at most 128 MiB of HBM per device.

v0:
```python
import jax
import jax.numpy as jnp
from jax import lax
from jax.sharding import PartitionSpec as P

BLK = 128


def local(tokens, enc_weight, enc_bias, dec_weight, dec_bias, slot_token, slot_latent, slot_count):
    block_size = BLK
    gathered = lax.all_gather(tokens, "dp", axis=0, tiled=True)
    total_rows = gathered.shape[0]
    features = tokens.shape[1]
    capacity = slot_token.shape[0]
    live_count = slot_count[0]

    def forward_slot(slot_index, carried):
        activations, partial_value = carried
        row_start = slot_token[slot_index] * block_size
        col_start = slot_latent[slot_index] * block_size
        tok_rows = lax.dynamic_slice_in_dim(gathered, row_start, block_size, 0)
        enc_block = lax.dynamic_slice_in_dim(enc_weight, col_start, block_size, 1)
        bias_block = lax.dynamic_slice_in_dim(enc_bias, col_start, block_size, 0)
        active = (
            jnp.dot(tok_rows, enc_block, preferred_element_type=jnp.float32) + bias_block[None, :]
        ).astype(jnp.bfloat16)
        dec_block = lax.dynamic_slice_in_dim(dec_weight, col_start, block_size, 0)
        contrib = jnp.dot(active, dec_block, preferred_element_type=jnp.float32)
        previous = lax.dynamic_slice_in_dim(partial_value, row_start, block_size, 0)
        partial_value = lax.dynamic_update_slice_in_dim(
            partial_value, previous + contrib, row_start, 0
        )
        activations = lax.dynamic_update_index_in_dim(activations, active, slot_index, 0)
        return (activations, partial_value)

    empty_acts = jnp.zeros((capacity, block_size, block_size), jnp.bfloat16)
    empty_sum = jnp.zeros((total_rows, features), jnp.float32)
    activations, partial_value = lax.fori_loop(0, live_count, forward_slot, (empty_acts, empty_sum))
    share = lax.psum_scatter(partial_value, ("dp", "latent"), scatter_dimension=0, tiled=True)
    share_rows = share.shape[0]
    offset = lax.axis_index("latent") * share_rows
    token_share = lax.dynamic_slice_in_dim(tokens, offset, share_rows, 0)
    residual = share + dec_bias[None, :] - token_share.astype(jnp.float32)
    scaled = residual * 0.25
    squared, dec_bias_grad = lax.psum(
        (jnp.sum(residual * residual), jnp.sum(scaled, axis=0)), ("dp", "latent")
    )
    grad_all = lax.all_gather(scaled.astype(jnp.bfloat16), ("dp", "latent"), axis=0, tiled=True)
    mean_error = squared / (total_rows * features)

    def backward_slot(slot_index, gradients):
        enc_acc, dec_acc, bias_acc = gradients
        row_start = slot_token[slot_index] * block_size
        col_start = slot_latent[slot_index] * block_size
        tok_rows = lax.dynamic_slice_in_dim(gathered, row_start, block_size, 0)
        grad_block = lax.dynamic_slice_in_dim(grad_all, row_start, block_size, 0)
        dec_block = lax.dynamic_slice_in_dim(dec_weight, col_start, block_size, 0)
        pre_grad = lax.dot_general(
            grad_block, dec_block, (((1,), (1,)), ((), ())), preferred_element_type=jnp.float32
        )
        old_bias = lax.dynamic_slice_in_dim(bias_acc, col_start, block_size, 0)
        bias_acc = lax.dynamic_update_slice_in_dim(
            bias_acc, old_bias + jnp.sum(pre_grad, axis=0), col_start, 0
        )
        pre_half = pre_grad.astype(jnp.bfloat16)
        enc_term = lax.dot_general(
            tok_rows, pre_half, (((0,), (0,)), ((), ())), preferred_element_type=jnp.float32
        )
        old_enc = lax.dynamic_slice_in_dim(enc_acc, col_start, block_size, 1)
        enc_acc = lax.dynamic_update_slice_in_dim(enc_acc, old_enc + enc_term, col_start, 1)
        dec_term = lax.dot_general(
            activations[slot_index],
            grad_block,
            (((0,), (0,)), ((), ())),
            preferred_element_type=jnp.float32,
        )
        old_dec = lax.dynamic_slice_in_dim(dec_acc, col_start, block_size, 0)
        dec_acc = lax.dynamic_update_slice_in_dim(dec_acc, old_dec + dec_term, col_start, 0)
        return (enc_acc, dec_acc, bias_acc)

    latents_here = enc_weight.shape[1]
    start_grads = (
        jnp.zeros((features, latents_here), jnp.float32),
        jnp.zeros((latents_here, features), jnp.float32),
        jnp.zeros((latents_here,), jnp.float32),
    )
    enc_acc, dec_acc, bias_acc = lax.fori_loop(0, live_count, backward_slot, start_grads)
    return (
        enc_acc.astype(jnp.bfloat16),
        dec_acc.astype(jnp.bfloat16),
        bias_acc,
        dec_bias_grad,
        mean_error,
    )


def solution(mesh):
    in_specs = (
        P("dp", None),
        P(None, ("dp", "latent")),
        P(("dp", "latent")),
        P(("dp", "latent"), None),
        P(),
        P(("dp", "latent")),
        P(("dp", "latent")),
        P(("dp", "latent")),
    )
    out_specs = (
        P(None, ("dp", "latent")),
        P(("dp", "latent"), None),
        P(("dp", "latent")),
        P(),
        P(),
    )
    return jax.shard_map(local, mesh=mesh, in_specs=in_specs, out_specs=out_specs, check_vma=False)
```

profile of v0, /device:TPU:10, one launch (start us, length us, event | category | flops | bytes accessed | tf_op | source)
XLA Modules:
  0.0 828.9 jit_solution(1080155368049432398)
XLA Ops:
  8.0 62.5 %all-gather.3.cloned.1.call-done = bf16[1024,1536]{1,0:T(8,128)(2,1)} async-done(((bf16[128,1536]{1,0:T(8,128)(2,1)}), bf16[1024,1536]{1,0:T(8,128)(2,1)}) %all-gather.3.cloned.1.call-update) | async-done | bytes 3145744 | tf_op jit(solution)/shard_map/all_gather | solution.py:11
  70.7 3.4 broadcast.5.clone
  74.1 247.6 %while.26 = (s32[]{:T(128)}, bf16[32,128,128]{2,1,0:T(8,128)(2,1)S(1)}, f32[1024,1536]{1,0:T(8,128)}, s32[]{:T(128)}, s32[32]{0:T(128)S(1)}, /*index=5*/bf16[102...) while((s32[]{:T(128)}, ...), condition=%wide.region_1.2_spmd, body=%wide.region_0.1_spmd.sunk | while | flops 100892688 | bytes 2852675 | solution.py:38
  280.1 2.4 fusion.35
  321.8 114.4 %reduce-scatter.2.cloned.1.call-done = f32[32,1536]{1,0:T(8,128)} async-done(((f32[1024,1536]{1,0:T(8,128)}), f32[32,1536]{1,0:T(8,128)}) %reduce-scatter.2.cloned.1.call-update) | async-done | bytes 196624 | tf_op jit(solution)/shard_map/reduce_scatter | solution.py:39
  438.5 40.0 %all-reduce = (f32[1536]{0:T(1024)}, f32[]{:T(128)}) all-reduce(f32[1536]{0:T(1024)S(1)} %get-tuple-element.125, f32[]{:T(128)} %get-tuple-element.124), channel_id=1, replica_groups=mesh['dp'=8,'latent'=4] {'dp','latent'}, use_global_device_ids=true, to_apply=%region_7.8 | all-reduce | flops 1537 | bytes 12296 | tf_op jit(solution)/shard_map/psum | solution.py:45
  479.2 17.8 %all-gather.5.cloned.1.call-done = bf16[1024,1536]{1,0:T(8,128)(2,1)} async-done(((bf16[32,1536]{1,0:T(8,128)(2,1)}), bf16[1024,1536]{1,0:T(8,128)(2,1)}) %all-gather.5.cloned.1.call-update) | async-done | bytes 3145744 | tf_op jit(solution)/shard_map/all_gather | solution.py:48
  497.0 3.4 broadcast.5
  500.4 3.4 broadcast_in_dim.15
  503.8 310.2 %while.27 = (s32[]{:T(128)}, f32[1536,1024]{1,0:T(8,128)}, f32[1024,1536]{1,0:T(8,128)}, f32[1024]{0:T(1024)S(1)}, s32[]{:T(128)}, /*index=5*/s32[32]{0:T(128)S(...) while((s32[]{:T(128)}, f32[1536,1024]{1,0:T(8,128)}, ...), condition=%wide.region_5.6_spmd, body=%wide.region_3.0_spmd.sunk | while | flops 151420944 | bytes 4819283 | solution.py:87
  508.6 2.5 fusion.41
  511.0 2.5 fusion.42
  518.2 2.5 fusion.41
  527.9 2.5 fusion.41
  530.4 2.4 fusion.42
  537.5 2.5 fusion.41
  540.1 2.5 fusion.42
  547.3 2.5 fusion.41
  549.8 2.5 fusion.42
  557.0 2.5 fusion.41
  559.5 2.5 fusion.42
  566.7 2.5 fusion.41
  569.2 2.5 fusion.42
  576.5 2.5 fusion.41
  586.1 2.5 fusion.41
  588.6 2.5 fusion.42
  595.8 2.5 fusion.41
  598.3 2.5 fusion.42
  605.5 2.5 fusion.41
  608.0 2.5 fusion.42
  615.2 2.5 fusion.41
  617.7 2.5 fusion.42
  624.9 2.5 fusion.41
  634.5 2.5 fusion.41
  644.2 2.5 fusion.41
  646.7 2.4 fusion.42
  653.8 2.5 fusion.41
  656.3 2.4 fusion.42
  663.5 2.5 fusion.41
  666.0 2.4 fusion.42
  673.2 2.5 fusion.41
  682.8 2.5 fusion.41
  692.5 2.5 fusion.41
  695.0 2.5 fusion.42
  702.2 2.5 fusion.41
  704.7 2.4 fusion.42
  711.8 2.5 fusion.41
  714.3 2.5 fusion.42
  721.5 2.5 fusion.41
  724.0 2.4 fusion.42
  731.2 2.5 fusion.41
  740.8 2.5 fusion.41
  743.3 2.5 fusion.42
  750.5 2.5 fusion.41
  753.0 2.5 fusion.42
  760.2 2.5 fusion.41
  769.8 2.5 fusion.41
  779.5 2.5 fusion.41
  781.9 2.5 fusion.42
  789.2 2.5 fusion.41
  798.8 2.5 fusion.41
  808.5 2.5 fusion.41
  811.0 2.4 fusion.42
  814.1 5.1 convert_element_type.20
  (318 shorter events, 301.2 us)
Async XLA Ops:
  7.2 67.0 %copy-start.3 = (s32[32]{0:T(128)S(1)}, s32[32]{0:T(128)}, u32[]{:S(2)}) copy-start(s32[32]{0:T(128)} %param.18) | copy-start | bytes 388
  7.2 67.0 %copy-start.4 = (s32[32]{0:T(128)S(1)}, s32[32]{0:T(128)}, u32[]{:S(2)}) copy-start(s32[32]{0:T(128)} %param.17) | copy-start | bytes 388
  7.2 63.3 %all-gather.3.cloned.1.call-start = ((), (), s32[]{:S(2)}) async-start(), calls=%async_computation.1 | async-start | bytes 3538944 | tf_op jit(solution)/shard_map/all_gather | solution.py:11
  7.9 428.3 %reduce-scatter.2.cloned.1.call-start = ((), (), s32[]{:S(2)}) async-start(), calls=%async_computation.2 | async-start | bytes 6488064 | tf_op jit(solution)/shard_map/reduce_scatter | solution.py:39
  321.7 114.5 %copy-start.2 = (f32[1536]{0:T(1024)S(1)}, f32[1536]{0:T(1024)}, u32[]{:S(2)}) copy-start(f32[1536]{0:T(1024)} %param.16) | copy-start | bytes 18436
  321.7 175.2 %all-gather.5.cloned.1.call-start = ((), (), s32[]{:S(2)}) async-start(), calls=%async_computation.3 | async-start | bytes 3244032 | tf_op jit(solution)/shard_map/all_gather | solution.py:48
  814.1 7.2 copy-start.1
  814.1 5.1 copy-start
Sparse Core Ops, SparseCore 0:
  10.2 60.2 all-gather.2
  321.8 114.3 reduce-scatter.1
  439.7 57.2 all-gather.4
where the time goes:
time: 837 us; the launch traced here: 829 us
  matrix products  324 us (39%)
  waiting for transfers between devices  195 us (23%)
  loops' own time  128 us (15%)
  local copies, waits for them, and re-layouts  110 us (13%)
  blocking collectives  40 us (5%)
  between operations  15.6 us (2%)
  other arithmetic  15.4 us (2%)
    reduce_scatter x1, waiting for transfers between devices, local(): lax.psum_scatter(partial_value, ('dp', 'latent'), scatter_dimension=0, ti...  114 us
    dot_general x32, matrix products, backward_slot(): lax.dot_general(tok_rows, pre_half, (((0,), (0,)), ((), ())), preferred_e...  79.7 us
    dot_general x32, matrix products, backward_slot(): lax.dot_general(activations[slot_index], grad_block, (((0,), (0,)), ((),...  78.2 us
    dot_general x32, matrix products, forward_slot(): contrib = jnp.dot(active, dec_block, preferred_element_type=jnp.float32)  77.1 us
    another operation x1, loops' own time, local(): lax.fori_loop(0, live_count, backward_slot, start_grads)  64.1 us
    another operation x1, loops' own time, local(): lax.fori_loop(0, live_count, forward_slot, (empty_acts, empty_sum))  64.1 us
    all_gather x1, waiting for transfers between devices, local(): gathered = lax.all_gather(tokens, 'dp', axis=0, tiled=True)  62.5 us
    dot_general x32, matrix products, backward_slot(): lax.dot_general(grad_block, dec_block, (((1,), (1,)), ((), ())), preferre...  44.6 us
  transfers between devices with their start and end apart: 3, of which 3 were waited for; matrix products, arithmetic and copies ran while one was open for 0% of the time, Pallas kernels for 0%

commit v1 on v0

v1 whole, which is shorter than its diff:
```python
import functools

import jax
import jax.numpy as jnp
from jax import lax
from jax.experimental import pallas as pl
from jax.experimental.pallas import tpu as pltpu
from jax.sharding import PartitionSpec as P

BLK = 128
MESH = pl.DeviceIdType.MESH
F32 = jnp.float32
BF16 = jnp.bfloat16
DMA = pltpu.SemaphoreType.DMA


def loop(low, high, body):
    def step(k, carry):
        body(k)
        return carry

    lax.fori_loop(low, high, step, jnp.int32(0))


class Place:
    def __init__(self, depth, width):
        self.depth, self.width = depth, width
        self.dp, self.lat = lax.axis_index("dp"), lax.axis_index("latent")
        self.z, self.x = self.dp // 2, self.dp % 2
        self.y, self.c = self.lat // 2, self.lat % 2
        self.ox, self.oc = 1 - self.x, 1 - self.c

    def zat(self, k):
        return (self.z + k) % self.depth

    def yat(self, j):
        return (self.y + j) % self.width

    def to_z(self, zz):
        return (zz * 2 + self.x, self.lat)

    def to_x(self):
        return (self.z * 2 + self.ox, self.lat)

    def to_y(self, yy):
        return (self.dp, yy * 2 + self.c)

    def to_c(self):
        return (self.dp, self.y * 2 + self.oc)

    def barrier(self):
        sem = pltpu.get_barrier_semaphore()
        peers = [self.to_z(self.zat(k)) for k in range(1, self.depth)]
        peers += [self.to_x()]
        peers += [self.to_y(self.yat(j)) for j in range(1, self.width)]
        peers += [self.to_c()]
        for peer in peers:
            pl.semaphore_signal(sem, inc=1, device_id=peer, device_id_type=MESH)
        pl.semaphore_wait(sem, len(peers))


def remote(src, dst, send, recv, peer):
    return pltpu.make_async_remote_copy(
        src_ref=src, dst_ref=dst, send_sem=send, recv_sem=recv, device_id=peer, device_id_type=MESH
    )


def gather_sems(depth, width):
    dps = depth * 2
    return [
        DMA((2, dps, width)),
        DMA((2, dps)),
        DMA((2, depth)),
        DMA((depth,)),
        DMA((dps, width)),
        DMA((depth, width)),
        DMA((depth, width)),
        DMA((2, dps)),
    ]


def gather(at, buf, sems):
    got, got_c, s_z, s_ax, s_ay, s_by, s_bx, s_c = sems
    depth, width = at.depth, at.width
    half = buf.shape[-1] // 2
    cols = (pl.ds(0, half), pl.ds(half, half))

    def shard(d, yy, h):
        return buf.at[d, yy, at.c, :, cols[h]]

    def copy(d, yy, h, send, peer):
        return remote(shard(d, yy, h), shard(d, yy, h), send, got.at[h, d, yy], peer)

    def core(d, h, cc):
        ref = buf.at[d, :, cc, :, cols[h]]
        return remote(ref, ref, s_c.at[h, d], got_c.at[h, d], at.to_c())

    def arrive(d, yy, h):
        copy(d, yy, h, s_z.at[h, 0], at.to_x()).wait_recv()

    def z_copy(k, h):
        return copy(at.dp, at.y, h, s_z.at[h, k], at.to_z(at.zat(k)))

    def ax(k):
        return copy(at.zat(k) * 2 + at.x, at.y, 0, s_ax.at[k], at.to_x())

    def ay(k, other, j):
        d = at.zat(k) * 2 + (at.ox if other else at.x)
        return copy(d, at.y, 0, s_ay.at[k * 2 + other, j], at.to_y(at.yat(j)))

    def by(k, j):
        return copy(at.zat(k) * 2 + at.x, at.y, 1, s_by.at[k, j], at.to_y(at.yat(j)))

    def bx(k, j):
        return copy(at.zat(k) * 2 + at.x, at.yat(j), 1, s_bx.at[k, j], at.to_x())

    def first(k):
        ax(k).start()
        for j in range(1, width):
            by(k, j).start()
        for j in range(1, width):
            ay(k, 0, j).start()
        bx(k, 0).start()

    for k in range(1, depth):
        for h in range(2):
            z_copy(k, h).start()
    first(0)

    def relay(k):
        for h in range(2):
            arrive(at.zat(k) * 2 + at.x, at.y, h)
        first(k)

    loop(1, depth, relay)

    def cross(k):
        d, od = at.zat(k) * 2 + at.x, at.zat(k) * 2 + at.ox
        arrive(od, at.y, 0)
        for j in range(1, width):
            ay(k, 1, j).start()
        for j in range(1, width):
            arrive(d, at.yat(j), 1)
            bx(k, j).start()
        core(d, 1, at.c).start()

    loop(0, depth, cross)

    def last(k):
        d, od = at.zat(k) * 2 + at.x, at.zat(k) * 2 + at.ox
        for dd in (d, od):
            for j in range(1, width):
                arrive(dd, at.yat(j), 0)
            core(dd, 0, at.c).start()
        for j in range(width):
            arrive(od, at.yat(j), 1)
        core(od, 1, at.c).start()

    loop(0, depth, last)

    def settle(k):
        d, od = at.zat(k) * 2 + at.x, at.zat(k) * 2 + at.ox
        for dd in (d, od):
            for h in range(2):
                core(dd, h, at.oc).wait_recv()
                core(dd, h, at.c).wait_send()
        ax(k).wait_send()
        bx(k, 0).wait_send()
        for j in range(1, width):
            ay(k, 0, j).wait_send()
            ay(k, 1, j).wait_send()
            by(k, j).wait_send()
            bx(k, j).wait_send()

    loop(0, depth, settle)
    for k in range(1, depth):
        for h in range(2):
            z_copy(k, h).wait_send()


def token_kernel(depth, width, tok_ref, buf, *sems):
    at = Place(depth, width)
    at.barrier()
    buf[at.dp, at.y, at.c] = tok_ref[at.y, at.c]
    gather(at, buf, sems)


def gather_tokens(tokens, depth, width):
    feats = tokens.shape[1]
    rows = tokens.shape[0] // (width * 2)
    vmem = pl.BlockSpec(memory_space=pltpu.VMEM)
    out = pl.pallas_call(
        functools.partial(token_kernel, depth, width),
        out_shape=jax.ShapeDtypeStruct((depth * 2, width, 2, rows, feats), BF16),
        in_specs=[vmem],
        out_specs=vmem,
        scratch_shapes=gather_sems(depth, width),
        compiler_params=pltpu.CompilerParams(
            collective_id=0, has_side_effects=True, vmem_limit_bytes=32 * 2 ** 20
        ),
        name="gather_tokens",
    )(tokens.reshape(width, 2, rows, feats))
    return out.reshape(-1, feats)


def reduce_kernel(depth, width, part, tok_ref, bias_ref, buf, stat_ref, *scratch):
    rc, a1, rya, a2a, rxa, rxb, a2b, ryb, a3, rz, tz, tx, ty, tc = scratch[:14]
    (s_c, g_c, s_ya, g_ya, s_xb, g_xb, s_xa, g_xa, s_yb, g_yb, s_z, g_z) = scratch[14:26]
    (s_tz, g_tz, s_tx, g_tx, s_ty, g_ty, s_tc, g_tc) = scratch[26:34]
    sems = scratch[34:]
    at = Place(depth, width)
    half = part.shape[-1] // 2
    low, high = pl.ds(0, half), pl.ds(half, half)
    at.barrier()

    def c_copy(d):
        return remote(part.at[d, :, at.oc], rc.at[d], s_c.at[d], g_c.at[d], at.to_c())

    def ya(d, j):
        yy = at.yat(j)
        return remote(a1.at[d, yy, :, low], rya.at[at.y, d], s_ya.at[d, j], g_ya.at[at.y, d], at.to_y(yy))

    def ya_in(d, yy):
        return remote(rya.at[yy, d], rya.at[yy, d], s_ya.at[d, 0], g_ya.at[yy, d], at.to_x())

    def xb(zz):
        return remote(a1.at[zz * 2 + at.ox, :, :, high], rxb.at[zz], s_xb.at[zz], g_xb.at[zz], at.to_x())

    def xa(zz):
        return remote(a2a.at[zz * 2 + at.ox], rxa.at[zz], s_xa.at[zz], g_xa.at[zz], at.to_x())

    def yb(zz, j):
        yy = at.yat(j)
        return remote(a2b.at[zz, yy], ryb.at[at.y, zz], s_yb.at[zz, j], g_yb.at[at.y, zz], at.to_y(yy))

    def yb_in(zz, yy):
        return remote(ryb.at[yy, zz], ryb.at[yy, zz], s_yb.at[zz, 0], g_yb.at[yy, zz], at.to_x())

    def zc(k):
        zz = at.zat(k)
        return remote(a3.at[zz], rz.at[at.z], s_z.at[k], g_z.at[at.z], at.to_z(zz))

    def z_in(zz):
        return remote(rz.at[zz], rz.at[zz], s_z.at[0], g_z.at[zz], at.to_x())

    def each(k):
        return at.zat(k + 1)

    def begin(k):
        c_copy(each(k) * 2 + at.ox).start()
        c_copy(each(k) * 2 + at.x).start()

    loop(0, depth, begin)

    def one(k):
        zz = each(k)
        for xx in (at.ox, at.x):
            d = zz * 2 + xx
            c_copy(d).wait_recv()
            a1[d] = (part[d, :, at.c].astype(F32) + rc[d].astype(F32)).astype(BF16)
            if xx is at.ox:
                xb(zz).start()
            for j in range(1, width):
                ya(d, j).start()

    loop(0, depth, one)

    def two(k):
        zz = each(k)
        for xx in (at.ox, at.x):
            d = zz * 2 + xx
            total = a1[d, at.y, :, low].astype(F32)
            for j in range(1, width):
                ya_in(d, at.yat(j)).wait_recv()
                total = total + rya[at.yat(j), d].astype(F32)
            a2a[d] = total.astype(BF16)
            if xx is at.ox:
                xa(zz).start()
        xb(zz).wait_recv()
        a2b[zz] = (a1[zz * 2 + at.x, :, :, high].astype(F32) + rxb[zz].astype(F32)).astype(BF16)
        for j in range(1, width):
            yb(zz, j).start()

    loop(0, depth, two)

    def sum_a(zz):
        xa(zz).wait_recv()
        return a2a[zz * 2 + at.x].astype(F32) + rxa[zz].astype(F32)

    def sum_b(zz):
        total = a2b[zz, at.y].astype(F32)
        for j in range(1, width):
            yb_in(zz, at.yat(j)).wait_recv()
            total = total + ryb[at.yat(j), zz].astype(F32)
        return total

    def three(k):
        zz = at.zat(k)
        a3[zz, :, low] = sum_a(zz).astype(BF16)
        a3[zz, :, high] = sum_b(zz).astype(BF16)
        zc(k).start()

    loop(1, depth, three)
    own = jnp.concatenate([sum_a(at.z), sum_b(at.z)], axis=-1)
    for k in range(1, depth):
        zz = at.zat(k)
        z_in(zz).wait_recv()
        own = own + rz[zz].astype(F32)
    residual = own + bias_ref[...] - tok_ref[at.y, at.c].astype(F32)
    scaled = residual * 0.25
    buf[at.dp, at.y, at.c] = scaled.astype(BF16)
    tz[at.z, 0:1, :] = jnp.sum(scaled, axis=0, keepdims=True)
    tz[at.z, 1:2, :] = jnp.sum(residual * residual, axis=0, keepdims=True)

    def tz_copy(k):
        return remote(tz.at[at.z], tz.at[at.z], s_tz.at[k], g_tz.at[at.z], at.to_z(at.zat(k)))

    def tz_in(zz):
        return remote(tz.at[zz], tz.at[zz], s_tz.at[0], g_tz.at[zz], at.to_x())

    for k in range(1, depth):
        tz_copy(k).start()
    gather(at, buf, sems)
    for k in range(1, depth):
        tz_in(at.zat(k)).wait_recv()
    tx[at.x] = jnp.sum(tz[...], axis=0)
    x_stat = remote(tx.at[at.x], tx.at[at.x], s_tx, g_tx, at.to_x())
    x_stat.start()
    x_stat.wait_recv()
    ty[at.y] = tx[0] + tx[1]

    def ty_copy(j):
        return remote(ty.at[at.y], ty.at[at.y], s_ty.at[j], g_ty.at[at.y], at.to_y(at.yat(j)))

    for j in range(1, width):
        ty_copy(j).start()
    for j in range(1, width):
        yy = at.yat(j)
        remote(ty.at[yy], ty.at[yy], s_ty.at[0], g_ty.at[yy], at.to_x()).wait_recv()
    tc[at.c] = jnp.sum(ty[...], axis=0)
    c_stat = remote(tc.at[at.c], tc.at[at.c], s_tc, g_tc, at.to_c())
    c_stat.start()
    c_stat.wait_recv()
    stat_ref[...] = tc[0] + tc[1]

    x_stat.wait_send()
    c_stat.wait_send()
    for j in range(1, width):
        ty_copy(j).wait_send()
    for k in range(1, depth):
        tz_copy(k).wait_send()
        zc(k).wait_send()

    def settle(k):
        zz = each(k)
        for xx in (at.ox, at.x):
            d = zz * 2 + xx
            c_copy(d).wait_send()
            for j in range(1, width):
                ya(d, j).wait_send()
        xb(zz).wait_send()
        xa(zz).wait_send()
        for j in range(1, width):
            yb(zz, j).wait_send()

    loop(0, depth, settle)


def reduce_gather(partial_value, tokens, dec_bias, depth, width):
    feats = tokens.shape[1]
    rows = tokens.shape[0] // (width * 2)
    dps, half = depth * 2, feats // 2
    vmem = pl.BlockSpec(memory_space=pltpu.VMEM)
    block = pltpu.VMEM
    scratch = [
        block((dps, width, rows, feats), BF16),
        block((dps, width, rows, feats), BF16),
        block((width, dps, rows, half), BF16),
        block((dps, rows, half), BF16),
        block((depth, rows, half), BF16),
        block((depth, width, rows, half), BF16),
        block((depth, width, rows, half), BF16),
        block((width, depth, rows, half), BF16),
        block((depth, rows, feats), BF16),
        block((depth, rows, feats), BF16),
        block((depth, 2, feats), F32),
        block((2, 2, feats), F32),
        block((width, 2, feats), F32),
        block((2, 2, feats), F32),
        DMA((dps,)), DMA((dps,)),
        DMA((dps, width)), DMA((width, dps)),
        DMA((depth,)), DMA((depth,)),
        DMA((depth,)), DMA((depth,)),
        DMA((depth, width)), DMA((width, depth)),
        DMA((depth,)), DMA((depth,)),
        DMA((depth,)), DMA((depth,)),
        DMA, DMA,
        DMA((width,)), DMA((width,)),
        DMA, DMA,
    ] + gather_sems(depth, width)
    grads, stats = pl.pallas_call(
        functools.partial(reduce_kernel, depth, width),
        out_shape=(
            jax.ShapeDtypeStruct((dps, width, 2, rows, feats), BF16),
            jax.ShapeDtypeStruct((2, feats), F32),
        ),
        in_specs=[vmem] * 3,
        out_specs=(vmem, vmem),
        scratch_shapes=scratch,
        compiler_params=pltpu.CompilerParams(
            collective_id=1, has_side_effects=True, vmem_limit_bytes=48 * 2 ** 20
        ),
        name="reduce_gather",
    )(
        partial_value.reshape(dps, width, 2, rows, feats),
        tokens.reshape(width, 2, rows, feats),
        dec_bias.reshape(1, feats),
    )
    return grads.reshape(-1, feats), stats


def local(depth, width, tokens, enc_weight, enc_bias, dec_weight, dec_bias, slot_token, slot_latent, slot_count):
    feats = tokens.shape[1]
    latents = enc_weight.shape[1]
    total_rows = tokens.shape[0] * depth * 2
    t_blocks, l_blocks = total_rows // BLK, latents // BLK
    alive = jnp.arange(slot_token.shape[0], dtype=jnp.int32) < slot_count[0]
    at_token = (slot_token[:, None] == jnp.arange(t_blocks, dtype=jnp.int32)[None, :]) & alive[:, None]
    at_latent = slot_latent[:, None] == jnp.arange(l_blocks, dtype=jnp.int32)[None, :]
    live = jnp.any(at_token[:, :, None] & at_latent[:, None, :], axis=0)
    mask = jnp.broadcast_to(live[:, None, :, None], (t_blocks, BLK, l_blocks, BLK)).reshape(total_rows, latents)

    gathered = gather_tokens(tokens, depth, width)
    dense = jnp.dot(gathered, enc_weight, preferred_element_type=F32) + enc_bias[None, :]
    active = jnp.where(mask, dense, 0.0).astype(BF16)
    partial_value = jnp.dot(active, dec_weight, preferred_element_type=F32).astype(BF16)
    grads, stats = reduce_gather(partial_value, tokens, dec_bias, depth, width)
    pre = lax.dot_general(grads, dec_weight, (((1,), (1,)), ((), ())), preferred_element_type=F32)
    pre = jnp.where(mask, pre, 0.0)
    bias_grad = jnp.sum(pre, axis=0)
    enc_grad = lax.dot_general(
        gathered, pre.astype(BF16), (((0,), (0,)), ((), ())), preferred_element_type=F32
    ).astype(BF16)
    dec_grad = lax.dot_general(active, grads, (((0,), (0,)), ((), ())), preferred_element_type=F32).astype(BF16)
    return enc_grad, dec_grad, bias_grad, stats[0], jnp.sum(stats[1]) / (total_rows * feats)


def solution(mesh):
    depth, width = mesh.shape["dp"] // 2, mesh.shape["latent"] // 2
    in_specs = (
        P("dp", None),
        P(None, ("dp", "latent")),
        P(("dp", "latent")),
        P(("dp", "latent"), None),
        P(),
        P(("dp", "latent")),
        P(("dp", "latent")),
        P(("dp", "latent")),
    )
    out_specs = (
        P(None, ("dp", "latent")),
        P(("dp", "latent"), None),
        P(("dp", "latent")),
        P(),
        P(),
    )
    return jax.shard_map(
        functools.partial(local, depth, width), mesh=mesh, in_specs=in_specs, out_specs=out_specs, check_vma=False
    )
```

time: 837 us -> 125 us (0.15)
  matrix products: 324 us -> 26 us
  waiting for transfers between devices: 195 us -> 0 us
  loops' own time: 128 us -> 0 us
  local copies, waits for them, and re-layouts: 110 us -> 8.63 us
  Pallas kernels: 0 us -> 84.5 us
  blocking collectives: 40 us -> 0 us
  other arithmetic: 15.4 us -> 1.75 us
  between operations: 15.6 us -> 3.39 us
    dot_general x160 -> x5, matrix products: 324 us -> 26 us  [the longest x1 7.81 us: local(): lax.dot_general(active, grads, (((0,), (0,)), ((), ())), preferred_elemen...]
    another operation x2 -> x0, loops' own time: 128 us -> none  [the longest x1 64.1 us: local(): lax.fori_loop(0, live_count, backward_slot, start_grads)]
    reduce_scatter x1 -> x0, waiting for transfers between devices: 114 us -> none  [local(): lax.psum_scatter(partial_value, ('dp', 'latent'), scatter_dimension=0, ti...]
    dynamic_slice x160 -> x0, local copies, waits for them, and re-layouts: 99.7 us -> none  [the longest x32 24.5 us: forward_slot(): bias_block = lax.dynamic_slice_in_dim(enc_bias, col_start, block_size, 0)]
    pallas_call x0 -> x2, Pallas kernels: none -> 84.5 us  [the longest x1 57.9 us: reduce_gather(): pl.pallas_call(functools.partial(reduce_kernel, depth, width), out_shape=...]
    all_gather x2 -> x0, waiting for transfers between devices: 80.2 us -> none  [the longest x1 62.5 us: local(): gathered = lax.all_gather(tokens, 'dp', axis=0, tiled=True)]
    psum x1 -> x0, blocking collectives: 40 us -> none  [local(): lax.psum((jnp.sum(residual * residual), jnp.sum(scaled, axis=0)), ('dp',...]
  transfers between devices with their start and end apart: 3 -> 0, of which waited for: 3 -> 0; matrix products, arithmetic and copies ran while one was open for 0% -> 0% of each run, Pallas kernels for 0% -> 0%
where the time goes in v1:
time: 125 us; the launch traced here: 124 us
  Pallas kernels  84.5 us (68%)
  matrix products  26 us (21%)
  local copies, waits for them, and re-layouts  8.63 us (7%)
  between operations  3.39 us (3%)
  other arithmetic  1.75 us (1%)
    pallas_call x1, Pallas kernels, reduce_gather(): pl.pallas_call(functools.partial(reduce_kernel, depth, width), out_shape=...  57.9 us
    pallas_call x1, Pallas kernels, gather_tokens(): pl.pallas_call(functools.partial(token_kernel, depth, width), out_shape=j...  26.6 us
    dot_general x1, matrix products, local(): lax.dot_general(active, grads, (((0,), (0,)), ((), ())), preferred_elemen...  7.81 us
    unnamed x25, local copies, waits for them, and re-layouts  7.59 us
    dot_general x1, matrix products, local(): lax.dot_general(gathered, pre.astype(BF16), (((0,), (0,)), ((), ())), pre...  5.07 us
    dot_general x1, matrix products, local(): jnp.dot(active, dec_weight, preferred_element_type=F32).astype(BF16)  4.77 us
    dot_general x1, matrix products, local(): lax.dot_general(grads, dec_weight, (((1,), (1,)), ((), ())), preferred_el...  4.51 us
    dot_general x1, matrix products, local(): jnp.dot(gathered, enc_weight, preferred_element_type=F32)  3.83 us

profile of v1, /device:TPU:10, one launch (start us, length us, event | category | flops | bytes accessed | tf_op | source)
XLA Modules:
  0.0 124.3 jit_solution(7878451381606224590)
XLA Ops:
  0.6 0.0 copy-start
  0.6 0.0 copy-start.10
  1.5 0.8 iota_compare_fusion
  2.3 0.2 and_reduce_fusion
  2.5 0.7 reshape.92.bias_ref
  3.2 0.3 broadcast_in_dim.6
  3.6 0.0 copy-start.7
  3.6 0.0 copy-start.3
  3.6 1.3 %copy-done.3 = bf16[128,1536]{1,0:T(8,128)(2,1)S(1)} copy-done((bf16[128,1536]{1,0:T(8,128)(2,1)S(1)}, bf16[128,1536]{1,0:T(8,128)(2,1)}, u32[]{:S(2)}) %copy-start.3) | copy-done | bytes 393240
  4.9 0.0 copy-start.9
  4.9 26.6 %gather_tokens.1 = bf16[8,2,2,32,1536]{4,3,2,1,0:T(8,128)(2,1)S(1)} custom-call(bf16[2,2,32,1536]{3,2,1,0:T(8,128)(2,1)S(1)} %bitcast.29), custom_call_target="tpu_custom_call" | custom-call | tf_op jit(solution)/shard_map/gather_tokens/pallas_call | solution.py:192
  31.5 0.0 copy-start.1
  31.5 0.0 copy-done.10
  31.5 0.0 copy-done.9
  31.5 3.8 %select_convert_fusion = bf16[1024,1024]{1,0:T(8,128)(2,1)S(1)} fusion(pred[128,8,8,128]{3,2,1,0:T(8,128)(4,1)S(1)} %bitcast.34, f32[1024]{0:T(1024)S(1)} %copy-done.10, bf16[1024,1536]{1,0:T(8,128)(2,1)S(1)} %bitcast.27, bf16[1536,1024]{1,0:T(8,128)(2,1)S(1)} %copy-done.9), kind=kOutput, calls=%fused_computation | convolution fusion | flops 3224371200 | bytes 9441280 | tf_op jit(solution)/shard_map/dot_general | solution.py:434
  35.4 0.0 copy-done.7
  35.4 0.0 copy-done.1
  35.4 0.0 copy-done
  35.4 0.0 copy-start.11
  35.4 0.0 copy-start.4
  35.4 4.8 %convolution_convert_fusion.2 = bf16[1024,1536]{1,0:T(8,128)(2,1)} fusion(bf16[1024,1024]{1,0:T(8,128)(2,1)S(1)} %select_convert_fusion, bf16[1024,1536]{1,0:T(8,128)(2,1)S(1)} %copy-done), kind=kOutput, calls=%fused_computation.4 | convolution fusion | flops 3222798336 | bytes 8388608 | tf_op jit(solution)/shard_map/dot_general | solution.py:436
  40.2 0.0 copy-done.11
  40.2 0.0 copy-done.4
  40.2 57.9 %reduce_gather.1 = (bf16[8,2,2,32,1536]{4,3,2,1,0:T(8,128)(2,1)S(1)}, f32[2,1536]{1,0:T(2,128)S(1)}) custom-call(bf16[8,2,2,32,1536]{4,3,2,1,0:T(8,128)(2,1)} %bitcast.33, bf16[2,2,32,1536]{3,2,1,0:T(8,128)(2,1)S(1)} %bitcast.30, f32[1,1536]{1,0:T(1,128)S(1)} %reshape.92.bias_ref), custom_call_target="tpu_custom_call" | custom-call | tf_op jit(solution)/shard_map/reduce_gather/pallas_call | solution.py:401
  98.1 0.0 copy-start.5
  98.1 1.6 %copy-done.5 = bf16[8,2,2,32,1536]{4,3,2,1,0:T(8,128)(2,1)} copy-done((bf16[8,2,2,32,1536]{4,3,2,1,0:T(8,128)(2,1)}, bf16[8,2,2,32,1536]{4,3,2,1,0:T(8,128)(2,1)S(1)}, u32[]{:S(2)}) %copy-start.5) | copy-done | bytes 3145752
  99.7 0.7 slice_reduce_fusion
  101.1 0.0 copy-start.6
  101.1 0.0 copy-start.8
  101.1 7.8 %convolution_convert_fusion = bf16[1024,1536]{1,0:T(8,128)(2,1)} fusion(bf16[1024,1024]{1,0:T(8,128)(2,1)} %copy-done.11, bf16[1024,1536]{1,0:T(8,128)(2,1)} %bitcast.31), kind=kOutput, calls=%fused_computation.2 | convolution fusion | flops 3222798336 | bytes 8388608 | tf_op jit(solution)/shard_map/dot_general | solution.py:444
  108.9 0.0 copy-done.6
  108.9 0.0 copy-done.8
  108.9 0.0 copy-start.2
  108.9 4.5 %fusion = (f32[1024]{0:T(1024)}, bf16[1024,1024]{1,0:T(8,128)(2,1)S(1)}) fusion(pred[128,8,8,128]{3,2,1,0:T(8,128)(4,1)S(1)} %bitcast.35, bf16[1024,1536]{1,0:T(8,128)(2,1)S(1)} %bitcast.32, bf16[1024,1536]{1,0:T(8,128)(2,1)S(1)} %copy-done), kind=kOutput, calls=%fused_computation.5 | convolution fusion | flops 3224370176 | bytes 9441280 | tf_op jit(solution)/shard_map/dot_general | solution.py:438
  113.4 0.0 copy-done.2
  113.4 5.1 %fusion.2 = bf16[1536,1024]{0,1:T(8,128)(2,1)} fusion(bf16[1024,1536]{1,0:T(8,128)(2,1)S(1)} %bitcast.28, bf16[1024,1024]{1,0:T(8,128)(2,1)S(1)} %get-tuple-element.22, pred[128,8,8,128]{3,2,1,0:T(8,128)(4,1)S(1)} %bitcast.36), kind=kOutput, calls=%fused_computation.7 | convolution fusion | flops 3223846912 | bytes 9437184 | tf_op jit(solution)/shard_map/dot_general | solution.py:441
  118.5 4.6 %copy.14 = bf16[1536,1024]{1,0:T(8,128)(2,1)} copy(bf16[1536,1024]{0,1:T(8,128)(2,1)} %fusion.2) | data formatting | bytes 6291456
  (1 shorter events, 0.0 us)
Async XLA Ops:
  0.6 34.7 %copy-start = (bf16[1024,1536]{1,0:T(8,128)(2,1)S(1)}, bf16[1024,1536]{1,0:T(8,128)(2,1)}, u32[]{:S(2)}) copy-start(bf16[1024,1536]{1,0:T(8,128)(2,1)} %param.11) | copy-start | bytes 9437188
  0.6 30.9 %copy-start.10 = (f32[1024]{0:T(1024)S(1)}, f32[1024]{0:T(1024)}, u32[]{:S(2)}) copy-start(f32[1024]{0:T(1024)} %param.10) | copy-start | bytes 12292
  3.6 31.8 %copy-start.7 = (pred[8,128,8,128]{3,2,1,0:T(8,128)(4,1)}, pred[8,128,8,128]{3,2,1,0:T(8,128)(4,1)S(1)}, u32[]{:S(2)}) copy-start(pred[8,128,8,128]{3,2,1,0:T(8,128)(4,1)S(1)} %broadcast_in_dim.6) | copy-start | bytes 3145732
  3.6 1.3 %copy-start.3 = (bf16[128,1536]{1,0:T(8,128)(2,1)S(1)}, bf16[128,1536]{1,0:T(8,128)(2,1)}, u32[]{:S(2)}) copy-start(bf16[128,1536]{1,0:T(8,128)(2,1)} %param.8) | copy-start | bytes 1179652
  4.9 26.6 %copy-start.9 = (bf16[1536,1024]{1,0:T(8,128)(2,1)S(1)}, bf16[1536,1024]{1,0:T(8,128)(2,1)}, u32[]{:S(2)}) copy-start(bf16[1536,1024]{1,0:T(8,128)(2,1)} %param.9) | copy-start | bytes 9437188
  31.5 3.9 %copy-start.1 = (bf16[8,2,2,32,1536]{4,3,2,1,0:T(8,128)(2,1)}, bf16[8,2,2,32,1536]{4,3,2,1,0:T(8,128)(2,1)S(1)}, u32[]{:S(2)}) copy-start(bf16[8,2,2,32,1536]{4,3,2,1,0:T(8,128)(2,1)S(1)} %gather_tokens.1) | copy-start | bytes 9437188
  35.4 4.8 %copy-start.11 = (bf16[1024,1024]{1,0:T(8,128)(2,1)}, bf16[1024,1024]{1,0:T(8,128)(2,1)S(1)}, u32[]{:S(2)}) copy-start(bf16[1024,1024]{1,0:T(8,128)(2,1)S(1)} %select_convert_fusion) | copy-start | bytes 6291460
  35.4 4.8 %copy-start.4 = (bf16[128,1536]{1,0:T(8,128)(2,1)S(1)}, bf16[128,1536]{1,0:T(8,128)(2,1)}, u32[]{:S(2)}) copy-start(bf16[128,1536]{1,0:T(8,128)(2,1)} %param.8) | copy-start | bytes 1179652
  98.1 1.6 %copy-start.5 = (bf16[8,2,2,32,1536]{4,3,2,1,0:T(8,128)(2,1)}, bf16[8,2,2,32,1536]{4,3,2,1,0:T(8,128)(2,1)S(1)}, u32[]{:S(2)}) copy-start(bf16[8,2,2,32,1536]{4,3,2,1,0:T(8,128)(2,1)S(1)} %get-tuple-element.7) | copy-start | bytes 9437188
  101.1 7.8 %copy-start.6 = (bf16[8,2,2,32,1536]{4,3,2,1,0:T(8,128)(2,1)S(1)}, bf16[8,2,2,32,1536]{4,3,2,1,0:T(8,128)(2,1)}, u32[]{:S(2)}) copy-start(bf16[8,2,2,32,1536]{4,3,2,1,0:T(8,128)(2,1)} %copy-done.5) | copy-start | bytes 9437188
  101.1 7.8 %copy-start.8 = (pred[8,128,8,128]{3,2,1,0:T(8,128)(4,1)S(1)}, pred[8,128,8,128]{3,2,1,0:T(8,128)(4,1)}, u32[]{:S(2)}) copy-start(pred[8,128,8,128]{3,2,1,0:T(8,128)(4,1)} %copy-done.7) | copy-start | bytes 3145732
  108.9 4.5 %copy-start.2 = (bf16[8,2,2,32,1536]{4,3,2,1,0:T(8,128)(2,1)S(1)}, bf16[8,2,2,32,1536]{4,3,2,1,0:T(8,128)(2,1)}, u32[]{:S(2)}) copy-start(bf16[8,2,2,32,1536]{4,3,2,1,0:T(8,128)(2,1)} %copy-done.1) | copy-start | bytes 9437188

commit v2 on v1

--- a/solution.py
+++ b/solution.py
@@ -69,17 +69,17 @@
     dps = depth * 2
     return [
         DMA((2, dps, width)),
-        DMA((2, dps)),
+        DMA((2, dps, width)),
         DMA((2, depth)),
         DMA((depth,)),
         DMA((dps, width)),
         DMA((depth, width)),
         DMA((depth, width)),
-        DMA((2, dps)),
+        DMA((2, dps, width)),
     ]
 
 
-def gather(at, buf, sems):
+def gather(at, buf, sems, hooks=()):
     got, got_c, s_z, s_ax, s_ay, s_by, s_bx, s_c = sems
     depth, width = at.depth, at.width
     half = buf.shape[-1] // 2
@@ -91,9 +91,9 @@
     def copy(d, yy, h, send, peer):
         return remote(shard(d, yy, h), shard(d, yy, h), send, got.at[h, d, yy], peer)
 
-    def core(d, h, cc):
-        ref = buf.at[d, :, cc, :, cols[h]]
-        return remote(ref, ref, s_c.at[h, d], got_c.at[h, d], at.to_c())
+    def core(d, yy, h, cc):
+        ref = buf.at[d, yy, cc, :, cols[h]]
+        return remote(ref, ref, s_c.at[h, d, yy], got_c.at[h, d, yy], at.to_c())
 
     def arrive(d, yy, h):
         copy(d, yy, h, s_z.at[h, 0], at.to_x()).wait_recv()
@@ -101,18 +101,23 @@
     def z_copy(k, h):
         return copy(at.dp, at.y, h, s_z.at[h, k], at.to_z(at.zat(k)))
 
+    def near(k):
+        return at.zat(k) * 2 + at.x
+
+    def far(k):
+        return at.zat(k) * 2 + at.ox
+
     def ax(k):
-        return copy(at.zat(k) * 2 + at.x, at.y, 0, s_ax.at[k], at.to_x())
+        return copy(near(k), at.y, 0, s_ax.at[k], at.to_x())
 
     def ay(k, other, j):
-        d = at.zat(k) * 2 + (at.ox if other else at.x)
-        return copy(d, at.y, 0, s_ay.at[k * 2 + other, j], at.to_y(at.yat(j)))
+        return copy(far(k) if other else near(k), at.y, 0, s_ay.at[k * 2 + other, j], at.to_y(at.yat(j)))
 
     def by(k, j):
-        return copy(at.zat(k) * 2 + at.x, at.y, 1, s_by.at[k, j], at.to_y(at.yat(j)))
+        return copy(near(k), at.y, 1, s_by.at[k, j], at.to_y(at.yat(j)))
 
     def bx(k, j):
-        return copy(at.zat(k) * 2 + at.x, at.yat(j), 1, s_bx.at[k, j], at.to_x())
+        return copy(near(k), at.yat(j), 1, s_bx.at[k, j], at.to_x())
 
     def first(k):
         ax(k).start()
@@ -121,6 +126,27 @@
         for j in range(1, width):
             ay(k, 0, j).start()
         bx(k, 0).start()
+        for h in range(2):
+            core(near(k), at.y, h, at.c).start()
+
+    def cross(k):
+        arrive(far(k), at.y, 0)
+        for j in range(1, width):
+            ay(k, 1, j).start()
+        core(far(k), at.y, 0, at.c).start()
+        for j in range(1, width):
+            arrive(near(k), at.yat(j), 1)
+            bx(k, j).start()
+            core(near(k), at.yat(j), 1, at.c).start()
+
+    def last(k):
+        for dd in (near(k), far(k)):
+            for j in range(1, width):
+                arrive(dd, at.yat(j), 0)
+                core(dd, at.yat(j), 0, at.c).start()
+        for j in range(width):
+            arrive(far(k), at.yat(j), 1)
+            core(far(k), at.yat(j), 1, at.c).start()
 
     for k in range(1, depth):
         for h in range(2):
@@ -129,41 +155,26 @@
 
     def relay(k):
         for h in range(2):
-            arrive(at.zat(k) * 2 + at.x, at.y, h)
+            arrive(near(k), at.y, h)
         first(k)
+        cross(k - 1)
 
     loop(1, depth, relay)
-
-    def cross(k):
-        d, od = at.zat(k) * 2 + at.x, at.zat(k) * 2 + at.ox
-        arrive(od, at.y, 0)
-        for j in range(1, width):
-            ay(k, 1, j).start()
-        for j in range(1, width):
-            arrive(d, at.yat(j), 1)
-            bx(k, j).start()
-        core(d, 1, at.c).start()
-
-    loop(0, depth, cross)
-
-    def last(k):
-        d, od = at.zat(k) * 2 + at.x, at.zat(k) * 2 + at.ox
-        for dd in (d, od):
-            for j in range(1, width):
-                arrive(dd, at.yat(j), 0)
-            core(dd, 0, at.c).start()
-        for j in range(width):
-            arrive(od, at.yat(j), 1)
-        core(od, 1, at.c).start()
-
+    for hook in hooks[:1]:
+        hook()
+    cross(depth - 1)
+    for hook in hooks[1:2]:
+        hook()
     loop(0, depth, last)
+    for hook in hooks[2:3]:
+        hook()
 
     def settle(k):
-        d, od = at.zat(k) * 2 + at.x, at.zat(k) * 2 + at.ox
-        for dd in (d, od):
-            for h in range(2):
-                core(dd, h, at.oc).wait_recv()
-                core(dd, h, at.c).wait_send()
+        for dd in (near(k), far(k)):
+            for j in range(width):
+                for h in range(2):
+                    core(dd, at.yat(j), h, at.oc).wait_recv()
+                    core(dd, at.yat(j), h, at.c).wait_send()
         ax(k).wait_send()
         bx(k, 0).wait_send()
         for j in range(1, width):
@@ -188,6 +199,7 @@
 def gather_tokens(tokens, depth, width):
     feats = tokens.shape[1]
     rows = tokens.shape[0] // (width * 2)
+    whole = depth * 2 * tokens.size * 2
     vmem = pl.BlockSpec(memory_space=pltpu.VMEM)
     out = pl.pallas_call(
         functools.partial(token_kernel, depth, width),
@@ -196,7 +208,7 @@
         out_specs=vmem,
         scratch_shapes=gather_sems(depth, width),
         compiler_params=pltpu.CompilerParams(
-            collective_id=0, has_side_effects=True, vmem_limit_bytes=32 * 2 ** 20
+            collective_id=0, has_side_effects=True, vmem_limit_bytes=3 * whole + 2 ** 21
         ),
         name="gather_tokens",
     )(tokens.reshape(width, 2, rows, feats))
@@ -262,8 +274,6 @@
                 xb(zz).start()
             for j in range(1, width):
                 ya(d, j).start()
-
-    loop(0, depth, one)
 
     def two(k):
         zz = each(k)
@@ -281,8 +291,6 @@
         for j in range(1, width):
             yb(zz, j).start()
 
-    loop(0, depth, two)
-
     def sum_a(zz):
         xa(zz).wait_recv()
         return a2a[zz * 2 + at.x].astype(F32) + rxa[zz].astype(F32)
@@ -295,12 +303,23 @@
         return total
 
     def three(k):
-        zz = at.zat(k)
+        zz = each(k)
         a3[zz, :, low] = sum_a(zz).astype(BF16)
         a3[zz, :, high] = sum_b(zz).astype(BF16)
-        zc(k).start()
-
-    loop(1, depth, three)
+        zc(k + 1).start()
+
+    one(0)
+    one(1)
+    two(0)
+
+    def pipeline(k):
+        one(k)
+        two(k - 1)
+        three(k - 2)
+
+    loop(2, depth, pipeline)
+    two(depth - 1)
+    three(depth - 2)
     own = jnp.concatenate([sum_a(at.z), sum_b(at.z)], axis=-1)
     for k in range(1, depth):
         zz = at.zat(k)
@@ -320,26 +339,32 @@
 
     for k in range(1, depth):
         tz_copy(k).start()
-    gather(at, buf, sems)
-    for k in range(1, depth):
-        tz_in(at.zat(k)).wait_recv()
-    tx[at.x] = jnp.sum(tz[...], axis=0)
     x_stat = remote(tx.at[at.x], tx.at[at.x], s_tx, g_tx, at.to_x())
-    x_stat.start()
-    x_stat.wait_recv()
-    ty[at.y] = tx[0] + tx[1]
+    c_stat = remote(tc.at[at.c], tc.at[at.c], s_tc, g_tc, at.to_c())
 
     def ty_copy(j):
         return remote(ty.at[at.y], ty.at[at.y], s_ty.at[j], g_ty.at[at.y], at.to_y(at.yat(j)))
 
-    for j in range(1, width):
-        ty_copy(j).start()
-    for j in range(1, width):
-        yy = at.yat(j)
-        remote(ty.at[yy], ty.at[yy], s_ty.at[0], g_ty.at[yy], at.to_x()).wait_recv()
-    tc[at.c] = jnp.sum(ty[...], axis=0)
-    c_stat = remote(tc.at[at.c], tc.at[at.c], s_tc, g_tc, at.to_c())
-    c_stat.start()
+    def stat_x():
+        for k in range(1, depth):
+            tz_in(at.zat(k)).wait_recv()
+        tx[at.x] = jnp.sum(tz[...], axis=0)
+        x_stat.start()
+
+    def stat_y():
+        x_stat.wait_recv()
+        ty[at.y] = tx[0] + tx[1]
+        for j in range(1, width):
+            ty_copy(j).start()
+
+    def stat_c():
+        for j in range(1, width):
+            yy = at.yat(j)
+            remote(ty.at[yy], ty.at[yy], s_ty.at[0], g_ty.at[yy], at.to_x()).wait_recv()
+        tc[at.c] = jnp.sum(ty[...], axis=0)
+        c_stat.start()
+
+    gather(at, buf, sems, (stat_x, stat_y, stat_c))
     c_stat.wait_recv()
     stat_ref[...] = tc[0] + tc[1]
 
@@ -370,6 +395,7 @@
     feats = tokens.shape[1]
     rows = tokens.shape[0] // (width * 2)
     dps, half = depth * 2, feats // 2
+    whole = partial_value.size * 2
     vmem = pl.BlockSpec(memory_space=pltpu.VMEM)
     block = pltpu.VMEM
     scratch = [
@@ -408,7 +434,7 @@
         out_specs=(vmem, vmem),
         scratch_shapes=scratch,
         compiler_params=pltpu.CompilerParams(
-            collective_id=1, has_side_effects=True, vmem_limit_bytes=48 * 2 ** 20
+            collective_id=1, has_side_effects=True, vmem_limit_bytes=5 * whole + 2 ** 21
         ),
         name="reduce_gather",
     )(
@@ -417,6 +443,55 @@
         dec_bias.reshape(1, feats),
     )
     return grads.reshape(-1, feats), stats
+
+
+def backward_kernel(tok_ref, act_ref, grad_ref, dec_ref, live_ref, enc_out, dec_out, bias_out, flipped):
+    @pl.when(pl.program_id(0) == 0)
+    def _():
+        flipped[...] = tok_ref[...].T
+
+    pre = lax.dot_general(grad_ref[...], dec_ref[...], (((1,), (1,)), ((), ())), preferred_element_type=F32)
+    pieces = [
+        jnp.where(live_ref[t : t + 1, :] > 0, pre[t * BLK : (t + 1) * BLK], 0.0) for t in range(live_ref.shape[0])
+    ]
+    pre = jnp.concatenate(pieces, axis=0)
+    bias_out[...] = jnp.sum(pre, axis=0, keepdims=True)
+    enc_out[...] = jnp.dot(flipped[...], pre.astype(BF16), preferred_element_type=F32).astype(BF16)
+    dec_out[...] = lax.dot_general(
+        act_ref[...], grad_ref[...], (((0,), (0,)), ((), ())), preferred_element_type=F32
+    ).astype(BF16)
+
+
+def backward(gathered, active, grads, dec_weight, live):
+    rows, feats = gathered.shape
+    latents = dec_weight.shape[0]
+    tile = 2 * BLK
+    live_cols = jnp.repeat(live.astype(F32), BLK, axis=1)
+    vmem = pl.BlockSpec(memory_space=pltpu.VMEM)
+    return pl.pallas_call(
+        backward_kernel,
+        grid=(latents // tile,),
+        out_shape=(
+            jax.ShapeDtypeStruct((feats, latents), BF16),
+            jax.ShapeDtypeStruct((latents, feats), BF16),
+            jax.ShapeDtypeStruct((1, latents), F32),
+        ),
+        in_specs=[
+            vmem,
+            pl.BlockSpec((rows, tile), lambda i: (0, i)),
+            vmem,
+            pl.BlockSpec((tile, feats), lambda i: (i, 0)),
+            pl.BlockSpec((live.shape[0], tile), lambda i: (0, i)),
+        ],
+        out_specs=(
+            pl.BlockSpec((feats, tile), lambda i: (0, i)),
+            pl.BlockSpec((tile, feats), lambda i: (i, 0)),
+            pl.BlockSpec((1, tile), lambda i: (0, i)),
+        ),
+        scratch_shapes=[pltpu.VMEM((feats, rows), BF16)],
+        compiler_params=pltpu.CompilerParams(vmem_limit_bytes=10 * rows * feats),
+        name="backward",
+    )(gathered, active, grads, dec_weight, live_cols)
 
 
 def local(depth, width, tokens, enc_weight, enc_bias, dec_weight, dec_bias, slot_token, slot_latent, slot_count):
@@ -435,14 +510,8 @@
     active = jnp.where(mask, dense, 0.0).astype(BF16)
     partial_value = jnp.dot(active, dec_weight, preferred_element_type=F32).astype(BF16)
     grads, stats = reduce_gather(partial_value, tokens, dec_bias, depth, width)
-    pre = lax.dot_general(grads, dec_weight, (((1,), (1,)), ((), ())), preferred_element_type=F32)
-    pre = jnp.where(mask, pre, 0.0)
-    bias_grad = jnp.sum(pre, axis=0)
-    enc_grad = lax.dot_general(
-        gathered, pre.astype(BF16), (((0,), (0,)), ((), ())), preferred_element_type=F32
-    ).astype(BF16)
-    dec_grad = lax.dot_general(active, grads, (((0,), (0,)), ((), ())), preferred_element_type=F32).astype(BF16)
-    return enc_grad, dec_grad, bias_grad, stats[0], jnp.sum(stats[1]) / (total_rows * feats)
+    enc_grad, dec_grad, bias_grad = backward(gathered, active, grads, dec_weight, live)
+    return enc_grad, dec_grad, bias_grad.reshape(latents), stats[0], jnp.sum(stats[1]) / (total_rows * feats)
 
 
 def solution(mesh):

time: 125 us -> 110 us (0.88)
  matrix products: 26 us -> 7.47 us
  Pallas kernels: 84.5 us -> 93.6 us
  local copies, waits for them, and re-layouts: 8.63 us -> 2.2 us
    pallas_call x0 -> x1, Pallas kernels: none -> 19 us  [backward(): pl.pallas_call(backward_kernel, grid=(latents // tile,), out_shape=(jax.S...]
    dot_general x3 -> x0, matrix products: 17.4 us -> none  [the longest x1 7.81 us: local(): lax.dot_general(active, grads, (((0,), (0,)), ((), ())), preferred_elemen...]
    pallas_call x1, Pallas kernels: 57.9 us -> 47.7 us  [reduce_gather(): pl.pallas_call(functools.partial(reduce_kernel, depth, width), out_shape=...]
    unnamed x25 -> x10, local copies, waits for them, and re-layouts: 7.59 us -> 1.02 us
where the time goes in v2:
time: 110 us; the launch traced here: 108 us
  Pallas kernels  93.6 us (85%)
  matrix products  7.47 us (7%)
  between operations  3.33 us (3%)
  local copies, waits for them, and re-layouts  2.2 us (2%)
  other arithmetic  1.77 us (2%)
    pallas_call x1, Pallas kernels, reduce_gather(): pl.pallas_call(functools.partial(reduce_kernel, depth, width), out_shape=...  47.7 us
    pallas_call x1, Pallas kernels, gather_tokens(): pl.pallas_call(functools.partial(token_kernel, depth, width), out_shape=j...  26.8 us
    pallas_call x1, Pallas kernels, backward(): pl.pallas_call(backward_kernel, grid=(latents // tile,), out_shape=(jax.S...  19 us
    dot_general x1, matrix products, local(): jnp.dot(gathered, enc_weight, preferred_element_type=F32)  3.83 us
    dot_general x1, matrix products, local(): jnp.dot(active, dec_weight, preferred_element_type=F32).astype(BF16)  3.64 us

profile of v2, /device:TPU:10, one launch (start us, length us, event | category | flops | bytes accessed | tf_op | source)
XLA Modules:
  0.0 108.3 jit_solution(11124914011949461534)
XLA Ops:
  0.6 0.0 copy-start
  0.6 0.0 copy-start.4
  1.5 0.8 iota_compare_fusion
  2.3 0.2 and_reduce_fusion
  2.5 0.1 copy.14
  2.6 0.7 reshape.98.bias_ref
  3.3 0.1 broadcast_bitcast_fusion.live_ref
  3.4 0.3 broadcast_in_dim.7
  3.7 0.0 copy-start.2
  3.7 1.0 copy-done.2
  4.7 26.8 %gather_tokens.1 = bf16[8,2,2,32,1536]{4,3,2,1,0:T(8,128)(2,1)S(1)} custom-call(bf16[2,2,32,1536]{3,2,1,0:T(8,128)(2,1)S(1)} %bitcast.21), custom_call_target="tpu_custom_call" | custom-call | tf_op jit(solution)/shard_map/gather_tokens/pallas_call | solution.py:204
  31.6 0.0 copy-done
  31.6 0.0 copy-done.4
  31.6 0.0 copy-start.1
  31.6 3.8 %select_convert_fusion.act_ref = bf16[1024,1024]{1,0:T(8,128)(2,1)S(1)} fusion(pred[128,8,8,128]{3,2,1,0:T(8,128)(4,1)S(1)} %bitcast.23, f32[1024]{0:T(1024)S(1)} %copy-done.4, bf16[1024,1536]{1,0:T(8,128)(2,1)S(1)} %bitcast.17, bf16[1536,1024]{1,0:T(8,128)(2,1)S(1)} %copy-done), kind=kOutput, calls=%fused_computation | convolution fusion | flops 3224371200 | bytes 9441280 | tf_op jit(solution)/shard_map/dot_general | solution.py:509
  35.4 0.0 copy-done.1
  35.4 0.0 copy-start.3
  35.5 3.6 %convolution_convert_fusion = bf16[1024,1536]{1,0:T(8,128)(2,1)S(1)} fusion(bf16[1024,1024]{1,0:T(8,128)(2,1)S(1)} %select_convert_fusion.act_ref, bf16[1024,1536]{1,0:T(8,128)(2,1)S(1)} %copy-done.1), kind=kOutput, calls=%fused_computation.1 | convolution fusion | flops 3222798336 | bytes 8388608 | tf_op jit(solution)/shard_map/dot_general | solution.py:511
  39.1 0.0 copy-done.3
  39.1 47.7 %reduce_gather.1 = (bf16[8,2,2,32,1536]{4,3,2,1,0:T(8,128)(2,1)S(1)}, f32[2,1536]{1,0:T(2,128)S(1)}) custom-call(bf16[8,2,2,32,1536]{4,3,2,1,0:T(8,128)(2,1)S(1)} %bitcast.20, bf16[2,2,32,1536]{3,2,1,0:T(8,128)(2,1)S(1)} %bitcast.22, f32[1,1536]{1,0:T(1,128)S(1)} %reshape.98.bias_ref), custom_call_target="tpu_custom_call" | custom-call | tf_op jit(solution)/shard_map/reduce_gather/pallas_call | solution.py:427
  86.9 19.0 %backward.1 = (bf16[1536,1024]{1,0:T(8,128)(2,1)}, bf16[1024,1536]{1,0:T(8,128)(2,1)}, f32[1,1024]{1,0:T(1,128)}) custom-call(bf16[1024,1536]{1,0:T(8,128)(2,1)S(1)} %bitcast.18, bf16[1024,1024]{1,0:T(8,128)(2,1)S(1)} %select_convert_fusion.act_ref, bf16[1024,1536]{1,0:T(8,128)(2,1)S(1)} %bitcast.19, bf16[1024,1536]{1,0:T(8,128)(2,1)S(1)} %copy-done.1, ...), custom_call_target="tpu_custom_call" | custom-call | tf_op jit(solution)/shard_map/backward/pallas_call | solution.py:471
  105.8 0.7 slice_reduce_fusion
  (2 shorter events, 0.0 us)
Async XLA Ops:
  0.6 30.9 %copy-start = (bf16[1536,1024]{1,0:T(8,128)(2,1)S(1)}, bf16[1536,1024]{1,0:T(8,128)(2,1)}, u32[]{:S(2)}) copy-start(bf16[1536,1024]{1,0:T(8,128)(2,1)} %param.9) | copy-start | bytes 9437188
  0.6 30.9 %copy-start.4 = (f32[1024]{0:T(1024)S(1)}, f32[1024]{0:T(1024)}, u32[]{:S(2)}) copy-start(f32[1024]{0:T(1024)} %param.10) | copy-start | bytes 12292
  3.7 1.0 copy-start.2
  31.6 3.8 %copy-start.1 = (bf16[1024,1536]{1,0:T(8,128)(2,1)S(1)}, bf16[1024,1536]{1,0:T(8,128)(2,1)}, u32[]{:S(2)}) copy-start(bf16[1024,1536]{1,0:T(8,128)(2,1)} %dec_ref.1) | copy-start | bytes 9437188
  35.4 3.7 %copy-start.3 = (bf16[128,1536]{1,0:T(8,128)(2,1)S(1)}, bf16[128,1536]{1,0:T(8,128)(2,1)}, u32[]{:S(2)}) copy-start(bf16[128,1536]{1,0:T(8,128)(2,1)} %param.8) | copy-start | bytes 1179652

commit v3 on v2

--- a/solution.py
+++ b/solution.py
@@ -79,7 +79,7 @@
     ]
 
 
-def gather(at, buf, sems, hooks=()):
+def gather(at, buf, sems, hooks=(), held=False):
     got, got_c, s_z, s_ax, s_ay, s_by, s_bx, s_c = sems
     depth, width = at.depth, at.width
     half = buf.shape[-1] // 2
@@ -119,13 +119,21 @@
     def bx(k, j):
         return copy(near(k), at.yat(j), 1, s_bx.at[k, j], at.to_x())
 
+    def mine(k):
+        return held and isinstance(k, int) and k == 0
+
     def first(k):
         ax(k).start()
-        for j in range(1, width):
-            by(k, j).start()
-        for j in range(1, width):
-            ay(k, 0, j).start()
+        if not mine(k):
+            for j in range(1, width):
+                by(k, j).start()
+            for j in range(1, width):
+                ay(k, 0, j).start()
         bx(k, 0).start()
+        if mine(k):
+            for j in range(1, width):
+                bx(k, j).start()
+            return
         for h in range(2):
             core(near(k), at.y, h, at.c).start()
 
@@ -134,13 +142,15 @@
         for j in range(1, width):
             ay(k, 1, j).start()
         core(far(k), at.y, 0, at.c).start()
+        if mine(k):
+            return
         for j in range(1, width):
             arrive(near(k), at.yat(j), 1)
             bx(k, j).start()
             core(near(k), at.yat(j), 1, at.c).start()
 
     def last(k):
-        for dd in (near(k), far(k)):
+        for dd in (far(k),) if mine(k) else (near(k), far(k)):
             for j in range(1, width):
                 arrive(dd, at.yat(j), 0)
                 core(dd, at.yat(j), 0, at.c).start()
@@ -157,20 +167,27 @@
         for h in range(2):
             arrive(near(k), at.y, h)
         first(k)
+
+    relay(1)
+    cross(0)
+
+    def both(k):
+        relay(k)
         cross(k - 1)
 
-    loop(1, depth, relay)
+    loop(2, depth, both)
     for hook in hooks[:1]:
         hook()
     cross(depth - 1)
     for hook in hooks[1:2]:
         hook()
-    loop(0, depth, last)
+    last(0)
+    loop(1, depth, last)
     for hook in hooks[2:3]:
         hook()
 
     def settle(k):
-        for dd in (near(k), far(k)):
+        for dd in (far(k),) if mine(k) else (near(k), far(k)):
             for j in range(width):
                 for h in range(2):
                     core(dd, at.yat(j), h, at.oc).wait_recv()
@@ -178,22 +195,26 @@
         ax(k).wait_send()
         bx(k, 0).wait_send()
         for j in range(1, width):
-            ay(k, 0, j).wait_send()
+            if not mine(k):
+                ay(k, 0, j).wait_send()
+                by(k, j).wait_send()
             ay(k, 1, j).wait_send()
-            by(k, j).wait_send()
             bx(k, j).wait_send()
 
-    loop(0, depth, settle)
+    settle(0)
+    loop(1, depth, settle)
     for k in range(1, depth):
         for h in range(2):
             z_copy(k, h).wait_send()
 
 
-def token_kernel(depth, width, tok_ref, buf, *sems):
+def token_kernel(depth, width, tok_ref, buf, load_sem, *sems):
     at = Place(depth, width)
+    load = pltpu.make_async_copy(tok_ref, buf.at[at.dp], load_sem)
+    load.start()
     at.barrier()
-    buf[at.dp, at.y, at.c] = tok_ref[at.y, at.c]
-    gather(at, buf, sems)
+    load.wait()
+    gather(at, buf, sems, held=True)
 
 
 def gather_tokens(tokens, depth, width):
@@ -204,9 +225,9 @@
     out = pl.pallas_call(
         functools.partial(token_kernel, depth, width),
         out_shape=jax.ShapeDtypeStruct((depth * 2, width, 2, rows, feats), BF16),
-        in_specs=[vmem],
+        in_specs=[pl.BlockSpec(memory_space=pl.ANY)],
         out_specs=vmem,
-        scratch_shapes=gather_sems(depth, width),
+        scratch_shapes=[DMA] + gather_sems(depth, width),
         compiler_params=pltpu.CompilerParams(
             collective_id=0, has_side_effects=True, vmem_limit_bytes=3 * whole + 2 ** 21
         ),
@@ -215,13 +236,13 @@
     return out.reshape(-1, feats)
 
 
-def reduce_kernel(depth, width, part, tok_ref, bias_ref, buf, stat_ref, *scratch):
+def reduce_kernel(depth, width, act_ref, dec_ref, tok_ref, bias_ref, buf, stat_ref, part, *scratch):
     rc, a1, rya, a2a, rxa, rxb, a2b, ryb, a3, rz, tz, tx, ty, tc = scratch[:14]
     (s_c, g_c, s_ya, g_ya, s_xb, g_xb, s_xa, g_xa, s_yb, g_yb, s_z, g_z) = scratch[14:26]
     (s_tz, g_tz, s_tx, g_tx, s_ty, g_ty, s_tc, g_tc) = scratch[26:34]
     sems = scratch[34:]
     at = Place(depth, width)
-    half = part.shape[-1] // 2
+    half = buf.shape[-1] // 2
     low, high = pl.ds(0, half), pl.ds(half, half)
     at.barrier()
 
@@ -259,10 +280,15 @@
         return at.zat(k + 1)
 
     def begin(k):
+        height = act_ref.shape[0] // depth
+        made = jnp.dot(
+            act_ref[pl.ds(pl.multiple_of(each(k) * height, height), height), :],
+            dec_ref[...],
+            preferred_element_type=F32,
+        )
+        part[pl.ds(each(k) * 2, 2)] = made.reshape((2,) + part.shape[1:]).astype(BF16)
         c_copy(each(k) * 2 + at.ox).start()
         c_copy(each(k) * 2 + at.x).start()
-
-    loop(0, depth, begin)
 
     def one(k):
         zz = each(k)
@@ -308,16 +334,23 @@
         a3[zz, :, high] = sum_b(zz).astype(BF16)
         zc(k + 1).start()
 
+    begin(0)
+    begin(1)
     one(0)
+    begin(2)
     one(1)
     two(0)
 
     def pipeline(k):
-        one(k)
-        two(k - 1)
-        three(k - 2)
-
-    loop(2, depth, pipeline)
+        begin(k)
+        one(k - 1)
+        two(k - 2)
+        three(k - 3)
+
+    loop(3, depth, pipeline)
+    one(depth - 1)
+    two(depth - 2)
+    three(depth - 3)
     two(depth - 1)
     three(depth - 2)
     own = jnp.concatenate([sum_a(at.z), sum_b(at.z)], axis=-1)
@@ -391,14 +424,15 @@
     loop(0, depth, settle)
 
 
-def reduce_gather(partial_value, tokens, dec_bias, depth, width):
+def reduce_gather(active, dec_weight, tokens, dec_bias, depth, width):
     feats = tokens.shape[1]
     rows = tokens.shape[0] // (width * 2)
     dps, half = depth * 2, feats // 2
-    whole = partial_value.size * 2
+    whole = active.shape[0] * feats * 2
     vmem = pl.BlockSpec(memory_space=pltpu.VMEM)
     block = pltpu.VMEM
     scratch = [
+        block((dps, width, 2, rows, feats), BF16),
         block((dps, width, rows, feats), BF16),
         block((dps, width, rows, feats), BF16),
         block((width, dps, rows, half), BF16),
@@ -430,15 +464,16 @@
             jax.ShapeDtypeStruct((dps, width, 2, rows, feats), BF16),
             jax.ShapeDtypeStruct((2, feats), F32),
         ),
-        in_specs=[vmem] * 3,
+        in_specs=[vmem] * 4,
         out_specs=(vmem, vmem),
         scratch_shapes=scratch,
         compiler_params=pltpu.CompilerParams(
-            collective_id=1, has_side_effects=True, vmem_limit_bytes=5 * whole + 2 ** 21
+            collective_id=1, has_side_effects=True, vmem_limit_bytes=7 * whole + 2 ** 22
         ),
         name="reduce_gather",
     )(
-        partial_value.reshape(dps, width, 2, rows, feats),
+        active,
+        dec_weight,
         tokens.reshape(width, 2, rows, feats),
         dec_bias.reshape(1, feats),
     )
@@ -508,8 +543,7 @@
     gathered = gather_tokens(tokens, depth, width)
     dense = jnp.dot(gathered, enc_weight, preferred_element_type=F32) + enc_bias[None, :]
     active = jnp.where(mask, dense, 0.0).astype(BF16)
-    partial_value = jnp.dot(active, dec_weight, preferred_element_type=F32).astype(BF16)
-    grads, stats = reduce_gather(partial_value, tokens, dec_bias, depth, width)
+    grads, stats = reduce_gather(active, dec_weight, tokens, dec_bias, depth, width)
     enc_grad, dec_grad, bias_grad = backward(gathered, active, grads, dec_weight, live)
     return enc_grad, dec_grad, bias_grad.reshape(latents), stats[0], jnp.sum(stats[1]) / (total_rows * feats)
 

time: 110 us -> 108 us (0.982)
  matrix products: 7.47 us -> 3.84 us
  Pallas kernels: 93.6 us -> 95.5 us
    dot_general x1 -> x0, matrix products: 3.64 us -> none  [local(): jnp.dot(active, dec_weight, preferred_element_type=F32).astype(BF16)]
    pallas_call x1, Pallas kernels: 47.7 us -> 49.5 us  [reduce_gather(): pl.pallas_call(functools.partial(reduce_kernel, depth, width), out_shape=...]
where the time goes in v3:
time: 108 us; the launch traced here: 107 us
  Pallas kernels  95.5 us (88%)
  matrix products  3.84 us (4%)
  between operations  3.32 us (3%)
  local copies, waits for them, and re-layouts  2.2 us (2%)
  other arithmetic  1.77 us (2%)
    pallas_call x1, Pallas kernels, reduce_gather(): pl.pallas_call(functools.partial(reduce_kernel, depth, width), out_shape=...  49.5 us
    pallas_call x1, Pallas kernels, gather_tokens(): pl.pallas_call(functools.partial(token_kernel, depth, width), out_shape=j...  27.1 us
    pallas_call x1, Pallas kernels, backward(): pl.pallas_call(backward_kernel, grid=(latents // tile,), out_shape=(jax.S...  19 us
    dot_general x1, matrix products, local(): jnp.dot(gathered, enc_weight, preferred_element_type=F32)  3.84 us

profile of v3, /device:TPU:10, one launch (start us, length us, event | category | flops | bytes accessed | tf_op | source)
XLA Modules:
  0.0 106.7 jit_solution(5953602526714669667)
XLA Ops:
  0.6 0.0 copy-start
  0.6 0.0 copy-start.4
  1.5 0.8 iota_compare_fusion
  2.3 0.2 and_reduce_fusion
  2.5 0.1 copy.14
  2.6 0.7 reshape.94.bias_ref
  3.3 0.1 broadcast_bitcast_fusion.live_ref
  3.4 0.3 broadcast_in_dim.7
  3.7 0.0 copy-start.2
  3.7 1.0 copy-done.2
  4.7 27.1 %gather_tokens.1 = bf16[8,2,2,32,1536]{4,3,2,1,0:T(8,128)(2,1)S(1)} custom-call(bf16[2,2,32,1536]{3,2,1,0:T(8,128)(2,1)S(1)} %bitcast.17), custom_call_target="tpu_custom_call" | custom-call | tf_op jit(solution)/shard_map/gather_tokens/pallas_call | solution.py:225
  31.8 0.0 copy-done
  31.8 0.0 copy-done.4
  31.9 0.0 copy-start.1
  31.9 0.0 copy-start.3
  31.9 3.8 %select_convert_fusion.act_ref = bf16[1024,1024]{1,0:T(8,128)(2,1)S(1)} fusion(pred[128,8,8,128]{3,2,1,0:T(8,128)(4,1)S(1)} %bitcast.19, f32[1024]{0:T(1024)S(1)} %copy-done.4, bf16[1024,1536]{1,0:T(8,128)(2,1)S(1)} %bitcast.14, bf16[1536,1024]{1,0:T(8,128)(2,1)S(1)} %copy-done), kind=kOutput, calls=%fused_computation | convolution fusion | flops 3224371200 | bytes 9441280 | tf_op jit(solution)/shard_map/dot_general | solution.py:544
  35.7 0.0 copy-done.1
  35.7 0.0 copy-done.3
  35.7 49.5 %reduce_gather.1 = (bf16[8,2,2,32,1536]{4,3,2,1,0:T(8,128)(2,1)S(1)}, f32[2,1536]{1,0:T(2,128)S(1)}) custom-call(bf16[1024,1024]{1,0:T(8,128)(2,1)S(1)} %select_convert_fusion.act_ref, bf16[1024,1536]{1,0:T(8,128)(2,1)S(1)} %copy-done.1, bf16[2,2,32,1536]{3,2,1,0:T(8,128)(2,1)S(1)} %bitcast.18, f32[1,1536]{1,0:T(1,128)S(1)} %reshape.94.bias_ref), custom_call_target="tpu_custom_call" | custom-call | tf_op jit(solution)/shard_map/reduce_gather/pallas_call | solution.py:461
  85.2 19.0 %backward.1 = (bf16[1536,1024]{1,0:T(8,128)(2,1)}, bf16[1024,1536]{1,0:T(8,128)(2,1)}, f32[1,1024]{1,0:T(1,128)}) custom-call(bf16[1024,1536]{1,0:T(8,128)(2,1)S(1)} %bitcast.15, bf16[1024,1024]{1,0:T(8,128)(2,1)S(1)} %select_convert_fusion.act_ref, bf16[1024,1536]{1,0:T(8,128)(2,1)S(1)} %bitcast.16, bf16[1024,1536]{1,0:T(8,128)(2,1)S(1)} %copy-done.1, ...), custom_call_target="tpu_custom_call" | custom-call | tf_op jit(solution)/shard_map/backward/pallas_call | solution.py:506
  104.2 0.7 slice_reduce_fusion
  (2 shorter events, 0.0 us)
Async XLA Ops:
  0.6 31.2 %copy-start = (bf16[1536,1024]{1,0:T(8,128)(2,1)S(1)}, bf16[1536,1024]{1,0:T(8,128)(2,1)}, u32[]{:S(2)}) copy-start(bf16[1536,1024]{1,0:T(8,128)(2,1)} %param.9) | copy-start | bytes 9437188
  0.6 31.2 %copy-start.4 = (f32[1024]{0:T(1024)S(1)}, f32[1024]{0:T(1024)}, u32[]{:S(2)}) copy-start(f32[1024]{0:T(1024)} %param.10) | copy-start | bytes 12292
  3.7 1.0 copy-start.2
  31.9 3.9 %copy-start.1 = (bf16[1024,1536]{1,0:T(8,128)(2,1)S(1)}, bf16[1024,1536]{1,0:T(8,128)(2,1)}, u32[]{:S(2)}) copy-start(bf16[1024,1536]{1,0:T(8,128)(2,1)} %dec_ref.3) | copy-start | bytes 9437188
  31.9 3.9 %copy-start.3 = (bf16[128,1536]{1,0:T(8,128)(2,1)S(1)}, bf16[128,1536]{1,0:T(8,128)(2,1)}, u32[]{:S(2)}) copy-start(bf16[128,1536]{1,0:T(8,128)(2,1)} %param.8) | copy-start | bytes 1179652
